TPU v7x, 32 devices: a whole 2x2x4 slice. The times are simulated.
32 devices in a mesh: gx: 2 (over x), gy: 4 (over y, core), gz: 4 (over z).
Axes of the slice: x: 2, y: 2, z: 4, core: 2. Of those that a mesh axis runs over, the one named last changes fastest.
Arguments:
- seed_cotangent: bfloat16 [2, 4, 4, 112, 2048], P('gx', 'gy', 'gz'), may hold values from -6 to 6
- trace_operator: bfloat16 [2, 4, 4, 2048, 2048], P('gx', 'gy', 'gz'), may hold values from -0.125 to 0.125
- face_matrices: bfloat16 [2, 4, 4, 6, 340, 340], P('gx', 'gy', 'gz'), may hold values from -0.3125 to 0.3125
- saved_traces: bfloat16 [2, 4, 4, 3, 112, 2048], P('gx', 'gy', 'gz'), may hold values from -6 to 6
- edge_flags: int32 [2, 4, 4, 6], P('gx', 'gy', 'gz'), may hold values 0 or 1
- node_map: int32 [2, 4, 4, 6, 340], P('gx', 'gy', 'gz'), may hold values from 0 to 339, each once within a row
Outputs:
- adjoint_traces: bfloat16 [2, 4, 4, 112, 2048], P('gx', 'gy', 'gz')
- face_gradient: bfloat16 [2, 4, 4, 6, 340, 340], P('gx', 'gy', 'gz')
Inputs may be any that keep to these rules, and one draw needn't show every extreme that they name: Each row node_map[.., k, :] names every face node once.
All inputs are finite; a program needn't handle non-finite values. No bound on the sum of `edge_flags` on one device may be relied on, other than what follows from the above.
Results may differ from a plain program's by a relative error of at most 0.0085.
Values may be sent and summed in bfloat16 or wider, within the bound.
A program may use at most 64 MiB of HBM per device.

v0:
```python
import math

import jax
import jax.numpy as jnp
from jax import lax
from jax.sharding import PartitionSpec as P


def with_halo(cells, sides, width):
    for axis, dim in sides:
        count = lax.axis_size(axis)
        ends = count - 1
        head = lax.slice_in_dim(cells, 0, width, axis=dim)
        tail = lax.slice_in_dim(cells, cells.shape[dim] - width, cells.shape[dim], axis=dim)
        cells = jnp.concatenate(
            [
                lax.ppermute(tail, axis, [(i, (i + 1) % count) for i in range(ends)]),
                cells,
                lax.ppermute(head, axis, [((i + 1) % count, i) for i in range(ends)]),
            ],
            axis=dim,
        )
    return cells


def face_block(array, number, width):
    return array[:, number * width : (number + 1) * width]


def axis_faces(block, width, axis_number):
    paired = jnp.stack([block[:, :width], block[:, width : 2 * width]], axis=0)
    if axis_number == 0:
        padded = with_halo(paired, (("gx", 0),), 1)
    elif axis_number == 1:
        padded = with_halo(paired, (("gy", 0),), 1)
    else:
        padded = with_halo(paired, (("gz", 0),), 1)
    return [padded[0], padded[3]]


def local(seed_cotangent, trace_operator, face_matrices, saved_traces, edge_flags, node_map):
    seeded = seed_cotangent[0, 0, 0].astype(jnp.float32)
    operator = trace_operator[0, 0, 0]
    matrices = face_matrices[0, 0, 0]
    stored = saved_traces[0, 0, 0]
    flagged = edge_flags[0, 0, 0]
    mapping = node_map[0, 0, 0]
    width = matrices.shape[-1]
    span = 6 * width
    sweeps = stored.shape[0]
    columns = seeded.shape[0]
    edge_mask = flagged[:, None, None] == 1
    node_ids = lax.broadcasted_iota(jnp.int32, (6, width, width), 1)
    selector = (mapping[:, None, :] == node_ids).astype(jnp.float32)
    placed = jnp.einsum(
        "kij,kjg->kig", selector.astype(jnp.bfloat16), matrices, preferred_element_type=jnp.float32
    ).astype(jnp.bfloat16)
    weights_used = jnp.where(edge_mask, matrices, placed)
    state = seeded
    inputs_kept = []
    saved_kept = []
    for sweep in range(sweeps):
        lowered = state.astype(jnp.bfloat16)
        pieces = []
        hidden = jnp.dot(lowered, operator, preferred_element_type=jnp.float32).astype(jnp.bfloat16)
        for axis_number in range(3):
            block = hidden[:, 2 * axis_number * width : (2 * axis_number + 2) * width]
            pieces = pieces + axis_faces(block, width, axis_number)
        received = jnp.stack(pieces, axis=0)
        own = jnp.stack([face_block(hidden, number, width) for number in range(6)], axis=0)
        inputs = jnp.where(edge_mask, own, received)
        fresh = jnp.einsum("kcf,kfg->kcg", inputs, weights_used, preferred_element_type=jnp.float32)
        state = (
            jnp.concatenate(
                [fresh[number] for number in range(6)] + [hidden[:, span:].astype(jnp.float32)],
                axis=1,
            )
            + seeded
        )
        earlier = stored[sweeps - 1 - sweep]
        stored_faces = jnp.stack(
            [face_block(earlier, number, width) for number in range(6)], axis=0
        )
        inputs_kept.append(inputs)
        saved_kept.append(stored_faces)
    gradient = jnp.einsum(
        "kcf,kcg->kfg",
        jnp.concatenate(inputs_kept, axis=1),
        jnp.concatenate(saved_kept, axis=1),
        preferred_element_type=jnp.float32,
    )
    permuted = jnp.einsum(
        "kij,kig->kjg",
        selector,
        gradient,
        precision=lax.Precision.HIGHEST,
        preferred_element_type=jnp.float32,
    )
    gradient = jnp.where(edge_mask, gradient, permuted)
    adjoint_traces = state.astype(jnp.bfloat16)
    face_gradient = (gradient * (1.0 / math.sqrt(columns))).astype(jnp.bfloat16)
    return (adjoint_traces[None, None, None], face_gradient[None, None, None])


def solution(mesh):
    return jax.shard_map(
        local,
        mesh=mesh,
        in_specs=(
            P("gx", "gy", "gz", None, None),
            P("gx", "gy", "gz", None, None),
            P("gx", "gy", "gz", None, None, None),
            P("gx", "gy", "gz", None, None, None),
            P("gx", "gy", "gz", None),
            P("gx", "gy", "gz", None, None),
        ),
        out_specs=(P("gx", "gy", "gz", None, None), P("gx", "gy", "gz", None, None, None)),
        check_vma=False,
    )
```

profile of v0, /device:TPU:1, one launch (start us, length us, event | category | flops | bytes accessed | tf_op | source)
XLA Modules:
  0.0 101.9 jit_solution(9500081039644034647)
XLA Ops:
  0.7 4.9 %fusion.7 = bf16[112,2048]{1,0:T(8,128)(2,1)S(1)} fusion(bf16[1,1,1,2048,2048]{4,3,2,1,0:T(8,128)(2,1)} %param.7, bf16[1,1,1,112,2048]{4,3,2,1,0:T(8,128)(2,1)} %param.6), kind=kOutput, calls=%fused_computation.10 | convolution fusion | flops 939753472 | bytes 9306112 | tf_op jit(solution)/shard_map/dot_general | solution.py:65
  5.8 1.3 %collective-permute-start.5 = (bf16[1,112,340]{2,1,0:T(8,128)(2,1)S(1)}, bf16[1,112,340]{2,1,0:T(8,128)(2,1)S(1)}, u32[]{:S(2)}, u32[]{:S(2)}) collective-permute-start(bf16[1,112,340]{2,1,0:T(8,128)(2,1)S(1)} %get-tuple-element.35), channel_id=1, source_target_pairs={{1,0},{2,1},{3,2},{5,4},{6,5},{7,6},{9,8},{10,9},{11,10},{13,12},{... | collective-permute-start | bytes 228488 | tf_op jit(solution)/shard_map/ppermute | solution.py:19
  7.1 4.7 %collective-permute-start.4 = (bf16[1,112,340]{2,1,0:T(8,128)(2,1)S(1)}, bf16[1,112,340]{2,1,0:T(8,128)(2,1)S(1)}, u32[]{:S(2)}, u32[]{:S(2)}) collective-permute-start(bf16[1,112,340]{2,1,0:T(8,128)(2,1)S(1)} %get-tuple-element.36), channel_id=1, source_target_pairs={{0,1},{1,2},{2,3},{4,5},{5,6},{6,7},{8,9},{9,10},{10,11},{12,13},{... | collective-permute-start | bytes 228488 | tf_op jit(solution)/shard_map/ppermute | solution.py:17
  11.7 4.4 %collective-permute-start.2 = (bf16[1,112,340]{2,1,0:T(8,128)(2,1)S(1)}, bf16[1,112,340]{2,1,0:T(8,128)(2,1)S(1)}, u32[]{:S(2)}, u32[]{:S(2)}) collective-permute-start(bf16[1,112,340]{2,1,0:T(8,128)(2,1)S(1)} %get-tuple-element.37), channel_id=1, source_target_pairs={{0,4},{4,8},{8,12},{1,5},{5,9},{9,13},{2,6},{6,10},{10,14},{3,7},{... | collective-permute-start | bytes 228488 | tf_op jit(solution)/shard_map/ppermute | solution.py:17
  16.2 1.9 %collective-permute-start.3 = (bf16[1,112,340]{2,1,0:T(8,128)(2,1)S(1)}, bf16[1,112,340]{2,1,0:T(8,128)(2,1)S(1)}, u32[]{:S(2)}, u32[]{:S(2)}) collective-permute-start(bf16[1,112,340]{2,1,0:T(8,128)(2,1)S(1)} %get-tuple-element.38), channel_id=1, source_target_pairs={{4,0},{8,4},{12,8},{5,1},{9,5},{13,9},{6,2},{10,6},{14,10},{7,3},{... | collective-permute-start | bytes 228488 | tf_op jit(solution)/shard_map/ppermute | solution.py:19
  18.1 3.1 %collective-permute-start = (bf16[1,112,340]{2,1,0:T(8,128)(2,1)S(1)}, bf16[1,112,340]{2,1,0:T(8,128)(2,1)S(1)}, u32[]{:S(2)}, u32[]{:S(2)}) collective-permute-start(bf16[1,112,340]{2,1,0:T(8,128)(2,1)S(1)} %get-tuple-element.39), channel_id=1, source_target_pairs={{0,16},{1,17},{2,18},{3,19},{4,20},{5,21},{6,22},{7,23},{8,24},{9,... | collective-permute-start | bytes 228488 | tf_op jit(solution)/shard_map/ppermute | solution.py:17
  25.4 2.3 %fusion.16 = bf16[6,340,340]{2,1,0:T(8,128)(2,1)S(1)} fusion(bf16[1,1,1,6,340,340]{5,4,3,2,1,0:T(8,128)(2,1)S(1)} %copy-done.8, s32[6,340]{1,0:T(8,128)S(1)} %bitcast.240, pred[6]{0:T(512)(128)(4,1)S(1)} %compare_bitcast_fusion), kind=kOutput, calls=%fused_computation.14 | convolution fusion | flops 475116000 | bytes 2782566 | tf_op jit(solution)/shard_map/kij,kjg->kig/dot_general | solution.py:55
  27.8 1.3 %collective-permute-start.1 = (bf16[1,112,340]{2,1,0:T(8,128)(2,1)S(1)}, bf16[1,112,340]{2,1,0:T(8,128)(2,1)S(1)}, u32[]{:S(2)}, u32[]{:S(2)}) collective-permute-start(bf16[1,112,340]{2,1,0:T(8,128)(2,1)S(1)} %get-tuple-element.40), channel_id=1, source_target_pairs={{16,0},{17,1},{18,2},{19,3},{20,4},{21,5},{22,6},{23,7},{24,8},{25... | collective-permute-start | bytes 228488 | tf_op jit(solution)/shard_map/ppermute | solution.py:19
  29.1 3.9 %collective-permute-done.1 = bf16[1,112,340]{2,1,0:T(8,128)(2,1)S(1)} collective-permute-done((bf16[1,112,340]{2,1,0:T(8,128)(2,1)S(1)}, bf16[1,112,340]{2,1,0:T(8,128)(2,1)S(1)}, u32[]{:S(2)}, u32[]{:S(2)}) %collective-permute-start.1) | collective-permute-done | bytes 76192 | tf_op jit(solution)/shard_map/ppermute | solution.py:19
  33.8 1.0 slice_bitcast_fusion.15
  34.8 1.7 %concatenate.74 = f32[1,1,1,112,2048]{4,3,2,1,0:T(8,128)S(1)} concatenate(f32[1,1,1,112,340]{4,3,2,1,0:T(8,128)} %get-tuple-element.22, f32[1,1,1,112,340]{4,3,2,1,0:T(8,128)} %get-tuple-element.21, f32[1,1,1,112,340]{4,3,2,1,0:T(8,128)} %get-tuple-element.20, f32[1,1,1,112,340]{4,3,2,1,0:T(8,128)} %get-tuple-element.19, f32[1,1,1,112,340]{4,3,2,1,0:T(8,128)} %get-tuple-element.18, ...), dimensions={4} | concatenate | bytes 1835008 | tf_op jit(solution)/shard_map/concatenate | solution.py:74
  36.5 4.7 %fusion.10 = bf16[112,2048]{1,0:T(8,128)(2,1)S(1)} fusion(bf16[1,1,1,2048,2048]{4,3,2,1,0:T(8,128)(2,1)} %param.7, f32[1,1,1,112,2048]{4,3,2,1,0:T(8,128)S(1)} %concatenate.74, bf16[1,1,1,112,2048]{4,3,2,1,0:T(8,128)(2,1)S(1)} %copy-done), kind=kOutput, calls=%fused_computation.11 | convolution fusion | flops 940441600 | bytes 10223616 | tf_op jit(solution)/shard_map/dot_general | solution.py:65
  42.0 1.6 %collective-permute-start.6 = (bf16[1,112,340]{2,1,0:T(8,128)(2,1)S(1)}, bf16[1,112,340]{2,1,0:T(8,128)(2,1)S(1)}, u32[]{:S(2)}, u32[]{:S(2)}) collective-permute-start(bf16[1,112,340]{2,1,0:T(8,128)(2,1)S(1)} %get-tuple-element.33), channel_id=1, source_target_pairs={{0,16},{1,17},{2,18},{3,19},{4,20},{5,21},{6,22},{7,23},{8,24},{9,... | collective-permute-start | bytes 228488 | tf_op jit(solution)/shard_map/ppermute | solution.py:17
  43.7 1.3 %collective-permute-start.11 = (bf16[1,112,340]{2,1,0:T(8,128)(2,1)S(1)}, bf16[1,112,340]{2,1,0:T(8,128)(2,1)S(1)}, u32[]{:S(2)}, u32[]{:S(2)}) collective-permute-start(bf16[1,112,340]{2,1,0:T(8,128)(2,1)S(1)} %get-tuple-element.29), channel_id=1, source_target_pairs={{1,0},{2,1},{3,2},{5,4},{6,5},{7,6},{9,8},{10,9},{11,10},{13,12},{... | collective-permute-start | bytes 228488 | tf_op jit(solution)/shard_map/ppermute | solution.py:19
  45.0 4.0 %collective-permute-start.10 = (bf16[1,112,340]{2,1,0:T(8,128)(2,1)S(1)}, bf16[1,112,340]{2,1,0:T(8,128)(2,1)S(1)}, u32[]{:S(2)}, u32[]{:S(2)}) collective-permute-start(bf16[1,112,340]{2,1,0:T(8,128)(2,1)S(1)} %get-tuple-element.30), channel_id=1, source_target_pairs={{0,1},{1,2},{2,3},{4,5},{5,6},{6,7},{8,9},{9,10},{10,11},{12,13},{... | collective-permute-start | bytes 228488 | tf_op jit(solution)/shard_map/ppermute | solution.py:17
  49.0 5.6 %collective-permute-start.8 = (bf16[1,112,340]{2,1,0:T(8,128)(2,1)S(1)}, bf16[1,112,340]{2,1,0:T(8,128)(2,1)S(1)}, u32[]{:S(2)}, u32[]{:S(2)}) collective-permute-start(bf16[1,112,340]{2,1,0:T(8,128)(2,1)S(1)} %get-tuple-element.31), channel_id=1, source_target_pairs={{0,4},{4,8},{8,12},{1,5},{5,9},{9,13},{2,6},{6,10},{10,14},{3,7},{... | collective-permute-start | bytes 228488 | tf_op jit(solution)/shard_map/ppermute | solution.py:17
  54.6 1.9 %collective-permute-start.9 = (bf16[1,112,340]{2,1,0:T(8,128)(2,1)S(1)}, bf16[1,112,340]{2,1,0:T(8,128)(2,1)S(1)}, u32[]{:S(2)}, u32[]{:S(2)}) collective-permute-start(bf16[1,112,340]{2,1,0:T(8,128)(2,1)S(1)} %get-tuple-element.32), channel_id=1, source_target_pairs={{4,0},{8,4},{12,8},{5,1},{9,5},{13,9},{6,2},{10,6},{14,10},{7,3},{... | collective-permute-start | bytes 228488 | tf_op jit(solution)/shard_map/ppermute | solution.py:19
  56.5 1.3 %collective-permute-start.7 = (bf16[1,112,340]{2,1,0:T(8,128)(2,1)S(1)}, bf16[1,112,340]{2,1,0:T(8,128)(2,1)S(1)}, u32[]{:S(2)}, u32[]{:S(2)}) collective-permute-start(bf16[1,112,340]{2,1,0:T(8,128)(2,1)S(1)} %get-tuple-element.34), channel_id=1, source_target_pairs={{16,0},{17,1},{18,2},{19,3},{20,4},{21,5},{22,6},{23,7},{24,8},{25... | collective-permute-start | bytes 228488 | tf_op jit(solution)/shard_map/ppermute | solution.py:19
  57.8 3.9 %collective-permute-done.7 = bf16[1,112,340]{2,1,0:T(8,128)(2,1)S(1)} collective-permute-done((bf16[1,112,340]{2,1,0:T(8,128)(2,1)S(1)}, bf16[1,112,340]{2,1,0:T(8,128)(2,1)S(1)}, u32[]{:S(2)}, u32[]{:S(2)}) %collective-permute-start.7) | collective-permute-done | bytes 76192 | tf_op jit(solution)/shard_map/ppermute | solution.py:19
  62.6 1.0 slice_bitcast_fusion.9
  63.6 1.7 %concatenate.83 = f32[1,1,1,112,2048]{4,3,2,1,0:T(8,128)S(1)} concatenate(f32[1,1,1,112,340]{4,3,2,1,0:T(8,128)} %get-tuple-element.16, f32[1,1,1,112,340]{4,3,2,1,0:T(8,128)} %get-tuple-element.15, f32[1,1,1,112,340]{4,3,2,1,0:T(8,128)} %get-tuple-element.14, f32[1,1,1,112,340]{4,3,2,1,0:T(8,128)} %get-tuple-element.13, f32[1,1,1,112,340]{4,3,2,1,0:T(8,128)} %get-tuple-element.12, ...), dimensions={4} | concatenate | bytes 1835008 | tf_op jit(solution)/shard_map/concatenate | solution.py:74
  65.3 4.7 %fusion.13 = bf16[112,2048]{1,0:T(8,128)(2,1)S(1)} fusion(bf16[1,1,1,2048,2048]{4,3,2,1,0:T(8,128)(2,1)} %param.7, f32[1,1,1,112,2048]{4,3,2,1,0:T(8,128)S(1)} %concatenate.83, bf16[1,1,1,112,2048]{4,3,2,1,0:T(8,128)(2,1)S(1)} %copy-done), kind=kOutput, calls=%fused_computation.12 | convolution fusion | flops 940441600 | bytes 10223616 | tf_op jit(solution)/shard_map/dot_general | solution.py:65
  70.8 1.5 %collective-permute-start.12 = (bf16[1,112,340]{2,1,0:T(8,128)(2,1)S(1)}, bf16[1,112,340]{2,1,0:T(8,128)(2,1)S(1)}, u32[]{:S(2)}, u32[]{:S(2)}) collective-permute-start(bf16[1,112,340]{2,1,0:T(8,128)(2,1)S(1)} %get-tuple-element.27), channel_id=1, source_target_pairs={{0,16},{1,17},{2,18},{3,19},{4,20},{5,21},{6,22},{7,23},{8,24},{9,... | collective-permute-start | bytes 228488 | tf_op jit(solution)/shard_map/ppermute | solution.py:17
  72.5 1.3 %collective-permute-start.17 = (bf16[1,112,340]{2,1,0:T(8,128)(2,1)S(1)}, bf16[1,112,340]{2,1,0:T(8,128)(2,1)S(1)}, u32[]{:S(2)}, u32[]{:S(2)}) collective-permute-start(bf16[1,112,340]{2,1,0:T(8,128)(2,1)S(1)} %get-tuple-element.23), channel_id=1, source_target_pairs={{1,0},{2,1},{3,2},{5,4},{6,5},{7,6},{9,8},{10,9},{11,10},{13,12},{... | collective-permute-start | bytes 228488 | tf_op jit(solution)/shard_map/ppermute | solution.py:19
  73.7 4.0 %collective-permute-start.16 = (bf16[1,112,340]{2,1,0:T(8,128)(2,1)S(1)}, bf16[1,112,340]{2,1,0:T(8,128)(2,1)S(1)}, u32[]{:S(2)}, u32[]{:S(2)}) collective-permute-start(bf16[1,112,340]{2,1,0:T(8,128)(2,1)S(1)} %get-tuple-element.24), channel_id=1, source_target_pairs={{0,1},{1,2},{2,3},{4,5},{5,6},{6,7},{8,9},{9,10},{10,11},{12,13},{... | collective-permute-start | bytes 228488 | tf_op jit(solution)/shard_map/ppermute | solution.py:17
  77.7 5.4 %collective-permute-start.14 = (bf16[1,112,340]{2,1,0:T(8,128)(2,1)S(1)}, bf16[1,112,340]{2,1,0:T(8,128)(2,1)S(1)}, u32[]{:S(2)}, u32[]{:S(2)}) collective-permute-start(bf16[1,112,340]{2,1,0:T(8,128)(2,1)S(1)} %get-tuple-element.25), channel_id=1, source_target_pairs={{0,4},{4,8},{8,12},{1,5},{5,9},{9,13},{2,6},{6,10},{10,14},{3,7},{... | collective-permute-start | bytes 228488 | tf_op jit(solution)/shard_map/ppermute | solution.py:17
  83.1 1.9 %collective-permute-start.15 = (bf16[1,112,340]{2,1,0:T(8,128)(2,1)S(1)}, bf16[1,112,340]{2,1,0:T(8,128)(2,1)S(1)}, u32[]{:S(2)}, u32[]{:S(2)}) collective-permute-start(bf16[1,112,340]{2,1,0:T(8,128)(2,1)S(1)} %get-tuple-element.26), channel_id=1, source_target_pairs={{4,0},{8,4},{12,8},{5,1},{9,5},{13,9},{6,2},{10,6},{14,10},{7,3},{... | collective-permute-start | bytes 228488 | tf_op jit(solution)/shard_map/ppermute | solution.py:19
  85.0 1.5 %collective-permute-start.13 = (bf16[1,112,340]{2,1,0:T(8,128)(2,1)S(1)}, bf16[1,112,340]{2,1,0:T(8,128)(2,1)S(1)}, u32[]{:S(2)}, u32[]{:S(2)}) collective-permute-start(bf16[1,112,340]{2,1,0:T(8,128)(2,1)S(1)} %get-tuple-element.28), channel_id=1, source_target_pairs={{16,0},{17,1},{18,2},{19,3},{20,4},{21,5},{22,6},{23,7},{24,8},{25... | collective-permute-start | bytes 228488 | tf_op jit(solution)/shard_map/ppermute | solution.py:19
  86.5 3.7 %collective-permute-done.13 = bf16[1,112,340]{2,1,0:T(8,128)(2,1)S(1)} collective-permute-done((bf16[1,112,340]{2,1,0:T(8,128)(2,1)S(1)}, bf16[1,112,340]{2,1,0:T(8,128)(2,1)S(1)}, u32[]{:S(2)}, u32[]{:S(2)}) %collective-permute-start.13) | collective-permute-done | bytes 76192 | tf_op jit(solution)/shard_map/ppermute | solution.py:19
  92.0 1.6 %concatenate.92 = f32[1,1,1,112,2048]{4,3,2,1,0:T(8,128)S(1)} concatenate(f32[1,1,1,112,340]{4,3,2,1,0:T(8,128)} %get-tuple-element.10, f32[1,1,1,112,340]{4,3,2,1,0:T(8,128)} %get-tuple-element.9, f32[1,1,1,112,340]{4,3,2,1,0:T(8,128)} %get-tuple-element.8, f32[1,1,1,112,340]{4,3,2,1,0:T(8,128)} %get-tuple-element.7, f32[1,1,1,112,340]{4,3,2,1,0:T(8,128)S(1)} %get-tuple-element.6, ...), dimensions={4} | concatenate | bytes 1835008 | tf_op jit(solution)/shard_map/concatenate | solution.py:74
  94.4 2.7 %fusion.20 = f32[6,340,340]{2,1,0:T(8,128)S(1)} fusion(bf16[6,112,340]{2,1,0:T(8,128)(2,1)S(1)} %broadcast_select_fusion, bf16[6,112,340]{2,1,0:T(8,128)(2,1)S(1)} %copy-done.2, bf16[6,112,340]{2,1,0:T(8,128)(2,1)S(1)} %broadcast_select_fusion.2, bf16[6,112,340]{2,1,0:T(8,128)(2,1)} %copy-done.5, bf16[6,112,340]{2,1,0:T(8,128)(2,1)} %copy-done.6, ...), kind=kOutput, calls=%fused_computation.18 | convolution fusion | flops 474324480 | bytes 5516160 | tf_op jit(solution)/shard_map/kcf,kcg->kfg/dot_general | solution.py:86
  97.1 4.8 %fusion.31 = bf16[1,1,1,6,340,340]{5,4,3,2,1,0:T(8,128)(2,1)} fusion(f32[6,340,340]{2,1,0:T(8,128)S(1)} %fusion.20, s32[6,340]{1,0:T(8,128)S(1)} %bitcast.241, pred[6]{0:T(512)(128)(4,1)S(1)} %compare_bitcast_fusion), kind=kOutput, calls=%fused_computation.29 | convolution fusion | flops 2832662528 | bytes 4169766 | tf_op jit(solution)/shard_map/kij,kig->kjg/dot_general | solution.py:92
  (105 shorter events, 10.0 us)
Async XLA Ops:
  0.6 20.7 %copy-start.9 = (s32[1,1,1,6]{3,2,1,0:T(1,128)S(1)}, s32[1,1,1,6]{3,2,1,0:T(1,128)}, u32[]{:S(2)}) copy-start(s32[1,1,1,6]{3,2,1,0:T(1,128)} %param.10) | copy-start | bytes 76
  0.6 20.7 %copy-start.7 = (s32[1,1,1,6,340]{4,2,3,1,0:T(1,128)S(1)}, s32[1,1,1,6,340]{4,2,3,1,0:T(1,128)}, u32[]{:S(2)}) copy-start(s32[1,1,1,6,340]{4,2,3,1,0:T(1,128)} %param.11) | copy-start | bytes 24484
  0.7 21.2 %copy-start.3 = (bf16[1,1,1,3,112,2048]{5,4,3,2,1,0:T(8,128)(2,1)S(1)}, bf16[1,1,1,3,112,2048]{5,4,3,2,1,0:T(8,128)(2,1)}, u32[]{:S(2)}) copy-start(bf16[1,1,1,3,112,2048]{5,4,3,2,1,0:T(8,128)(2,1)} %param.9) | copy-start | bytes 4128772
  5.8 27.3 %collective-permute-start.5 = (bf16[1,112,340]{2,1,0:T(8,128)(2,1)S(1)}, bf16[1,112,340]{2,1,0:T(8,128)(2,1)S(1)}, u32[]{:S(2)}, u32[]{:S(2)}) collective-permute-start(bf16[1,112,340]{2,1,0:T(8,128)(2,1)S(1)} %get-tuple-element.35), channel_id=1, source_target_pairs={{1,0},{2,1},{3,2},{5,4},{6,5},{7,6},{9,8},{10,9},{11,10},{13,12},{... | collective-permute-start | bytes 228488 | tf_op jit(solution)/shard_map/ppermute | solution.py:19
  7.1 26.0 %collective-permute-start.4 = (bf16[1,112,340]{2,1,0:T(8,128)(2,1)S(1)}, bf16[1,112,340]{2,1,0:T(8,128)(2,1)S(1)}, u32[]{:S(2)}, u32[]{:S(2)}) collective-permute-start(bf16[1,112,340]{2,1,0:T(8,128)(2,1)S(1)} %get-tuple-element.36), channel_id=1, source_target_pairs={{0,1},{1,2},{2,3},{4,5},{5,6},{6,7},{8,9},{9,10},{10,11},{12,13},{... | collective-permute-start | bytes 228488 | tf_op jit(solution)/shard_map/ppermute | solution.py:17
  11.7 21.3 %collective-permute-start.2 = (bf16[1,112,340]{2,1,0:T(8,128)(2,1)S(1)}, bf16[1,112,340]{2,1,0:T(8,128)(2,1)S(1)}, u32[]{:S(2)}, u32[]{:S(2)}) collective-permute-start(bf16[1,112,340]{2,1,0:T(8,128)(2,1)S(1)} %get-tuple-element.37), channel_id=1, source_target_pairs={{0,4},{4,8},{8,12},{1,5},{5,9},{9,13},{2,6},{6,10},{10,14},{3,7},{... | collective-permute-start | bytes 228488 | tf_op jit(solution)/shard_map/ppermute | solution.py:17
  16.2 16.8 %collective-permute-start.3 = (bf16[1,112,340]{2,1,0:T(8,128)(2,1)S(1)}, bf16[1,112,340]{2,1,0:T(8,128)(2,1)S(1)}, u32[]{:S(2)}, u32[]{:S(2)}) collective-permute-start(bf16[1,112,340]{2,1,0:T(8,128)(2,1)S(1)} %get-tuple-element.38), channel_id=1, source_target_pairs={{4,0},{8,4},{12,8},{5,1},{9,5},{13,9},{6,2},{10,6},{14,10},{7,3},{... | collective-permute-start | bytes 228488 | tf_op jit(solution)/shard_map/ppermute | solution.py:19
  18.1 9.6 %collective-permute-start = (bf16[1,112,340]{2,1,0:T(8,128)(2,1)S(1)}, bf16[1,112,340]{2,1,0:T(8,128)(2,1)S(1)}, u32[]{:S(2)}, u32[]{:S(2)}) collective-permute-start(bf16[1,112,340]{2,1,0:T(8,128)(2,1)S(1)} %get-tuple-element.39), channel_id=1, source_target_pairs={{0,16},{1,17},{2,18},{3,19},{4,20},{5,21},{6,22},{7,23},{8,24},{9,... | collective-permute-start | bytes 228488 | tf_op jit(solution)/shard_map/ppermute | solution.py:17
  21.6 3.7 %copy-start.8 = (bf16[1,1,1,6,340,340]{5,4,3,2,1,0:T(8,128)(2,1)S(1)}, bf16[1,1,1,6,340,340]{5,4,3,2,1,0:T(8,128)(2,1)}, u32[]{:S(2)}) copy-start(bf16[1,1,1,6,340,340]{5,4,3,2,1,0:T(8,128)(2,1)} %param.8) | copy-start | bytes 4161604
  23.0 0.8 copy-start.5
  23.8 0.8 copy-start.4
  24.6 0.8 copy-start.6
  27.8 5.2 %collective-permute-start.1 = (bf16[1,112,340]{2,1,0:T(8,128)(2,1)S(1)}, bf16[1,112,340]{2,1,0:T(8,128)(2,1)S(1)}, u32[]{:S(2)}, u32[]{:S(2)}) collective-permute-start(bf16[1,112,340]{2,1,0:T(8,128)(2,1)S(1)} %get-tuple-element.40), channel_id=1, source_target_pairs={{16,0},{17,1},{18,2},{19,3},{20,4},{21,5},{22,6},{23,7},{24,8},{25... | collective-permute-start | bytes 228488 | tf_op jit(solution)/shard_map/ppermute | solution.py:19
  33.3 3.2 %copy-start = (bf16[1,1,1,112,2048]{4,3,2,1,0:T(8,128)(2,1)S(1)}, bf16[1,1,1,112,2048]{4,3,2,1,0:T(8,128)(2,1)}, u32[]{:S(2)}) copy-start(bf16[1,1,1,112,2048]{4,3,2,1,0:T(8,128)(2,1)} %param.6) | copy-start | bytes 1376260
  42.0 14.5 %collective-permute-start.6 = (bf16[1,112,340]{2,1,0:T(8,128)(2,1)S(1)}, bf16[1,112,340]{2,1,0:T(8,128)(2,1)S(1)}, u32[]{:S(2)}, u32[]{:S(2)}) collective-permute-start(bf16[1,112,340]{2,1,0:T(8,128)(2,1)S(1)} %get-tuple-element.33), channel_id=1, source_target_pairs={{0,16},{1,17},{2,18},{3,19},{4,20},{5,21},{6,22},{7,23},{8,24},{9,... | collective-permute-start | bytes 228488 | tf_op jit(solution)/shard_map/ppermute | solution.py:17
  43.7 18.2 %collective-permute-start.11 = (bf16[1,112,340]{2,1,0:T(8,128)(2,1)S(1)}, bf16[1,112,340]{2,1,0:T(8,128)(2,1)S(1)}, u32[]{:S(2)}, u32[]{:S(2)}) collective-permute-start(bf16[1,112,340]{2,1,0:T(8,128)(2,1)S(1)} %get-tuple-element.29), channel_id=1, source_target_pairs={{1,0},{2,1},{3,2},{5,4},{6,5},{7,6},{9,8},{10,9},{11,10},{13,12},{... | collective-permute-start | bytes 228488 | tf_op jit(solution)/shard_map/ppermute | solution.py:19
  45.0 16.9 %collective-permute-start.10 = (bf16[1,112,340]{2,1,0:T(8,128)(2,1)S(1)}, bf16[1,112,340]{2,1,0:T(8,128)(2,1)S(1)}, u32[]{:S(2)}, u32[]{:S(2)}) collective-permute-start(bf16[1,112,340]{2,1,0:T(8,128)(2,1)S(1)} %get-tuple-element.30), channel_id=1, source_target_pairs={{0,1},{1,2},{2,3},{4,5},{5,6},{6,7},{8,9},{9,10},{10,11},{12,13},{... | collective-permute-start | bytes 228488 | tf_op jit(solution)/shard_map/ppermute | solution.py:17
  49.0 12.8 %collective-permute-start.8 = (bf16[1,112,340]{2,1,0:T(8,128)(2,1)S(1)}, bf16[1,112,340]{2,1,0:T(8,128)(2,1)S(1)}, u32[]{:S(2)}, u32[]{:S(2)}) collective-permute-start(bf16[1,112,340]{2,1,0:T(8,128)(2,1)S(1)} %get-tuple-element.31), channel_id=1, source_target_pairs={{0,4},{4,8},{8,12},{1,5},{5,9},{9,13},{2,6},{6,10},{10,14},{3,7},{... | collective-permute-start | bytes 228488 | tf_op jit(solution)/shard_map/ppermute | solution.py:17
  54.6 7.2 %collective-permute-start.9 = (bf16[1,112,340]{2,1,0:T(8,128)(2,1)S(1)}, bf16[1,112,340]{2,1,0:T(8,128)(2,1)S(1)}, u32[]{:S(2)}, u32[]{:S(2)}) collective-permute-start(bf16[1,112,340]{2,1,0:T(8,128)(2,1)S(1)} %get-tuple-element.32), channel_id=1, source_target_pairs={{4,0},{8,4},{12,8},{5,1},{9,5},{13,9},{6,2},{10,6},{14,10},{7,3},{... | collective-permute-start | bytes 228488 | tf_op jit(solution)/shard_map/ppermute | solution.py:19
  56.5 5.2 %collective-permute-start.7 = (bf16[1,112,340]{2,1,0:T(8,128)(2,1)S(1)}, bf16[1,112,340]{2,1,0:T(8,128)(2,1)S(1)}, u32[]{:S(2)}, u32[]{:S(2)}) collective-permute-start(bf16[1,112,340]{2,1,0:T(8,128)(2,1)S(1)} %get-tuple-element.34), channel_id=1, source_target_pairs={{16,0},{17,1},{18,2},{19,3},{20,4},{21,5},{22,6},{23,7},{24,8},{25... | collective-permute-start | bytes 228488 | tf_op jit(solution)/shard_map/ppermute | solution.py:19
  62.1 1.5 %copy-start.1 = (bf16[6,112,340]{2,1,0:T(8,128)(2,1)}, bf16[6,112,340]{2,1,0:T(8,128)(2,1)S(1)}, u32[]{:S(2)}) copy-start(bf16[6,112,340]{2,1,0:T(8,128)(2,1)S(1)} %broadcast_select_fusion.1) | copy-start | bytes 1370884
  70.8 14.2 %collective-permute-start.12 = (bf16[1,112,340]{2,1,0:T(8,128)(2,1)S(1)}, bf16[1,112,340]{2,1,0:T(8,128)(2,1)S(1)}, u32[]{:S(2)}, u32[]{:S(2)}) collective-permute-start(bf16[1,112,340]{2,1,0:T(8,128)(2,1)S(1)} %get-tuple-element.27), channel_id=1, source_target_pairs={{0,16},{1,17},{2,18},{3,19},{4,20},{5,21},{6,22},{7,23},{8,24},{9,... | collective-permute-start | bytes 228488 | tf_op jit(solution)/shard_map/ppermute | solution.py:17
  72.5 17.9 %collective-permute-start.17 = (bf16[1,112,340]{2,1,0:T(8,128)(2,1)S(1)}, bf16[1,112,340]{2,1,0:T(8,128)(2,1)S(1)}, u32[]{:S(2)}, u32[]{:S(2)}) collective-permute-start(bf16[1,112,340]{2,1,0:T(8,128)(2,1)S(1)} %get-tuple-element.23), channel_id=1, source_target_pairs={{1,0},{2,1},{3,2},{5,4},{6,5},{7,6},{9,8},{10,9},{11,10},{13,12},{... | collective-permute-start | bytes 228488 | tf_op jit(solution)/shard_map/ppermute | solution.py:19
  73.7 16.6 %collective-permute-start.16 = (bf16[1,112,340]{2,1,0:T(8,128)(2,1)S(1)}, bf16[1,112,340]{2,1,0:T(8,128)(2,1)S(1)}, u32[]{:S(2)}, u32[]{:S(2)}) collective-permute-start(bf16[1,112,340]{2,1,0:T(8,128)(2,1)S(1)} %get-tuple-element.24), channel_id=1, source_target_pairs={{0,1},{1,2},{2,3},{4,5},{5,6},{6,7},{8,9},{9,10},{10,11},{12,13},{... | collective-permute-start | bytes 228488 | tf_op jit(solution)/shard_map/ppermute | solution.py:17
  77.7 12.6 %collective-permute-start.14 = (bf16[1,112,340]{2,1,0:T(8,128)(2,1)S(1)}, bf16[1,112,340]{2,1,0:T(8,128)(2,1)S(1)}, u32[]{:S(2)}, u32[]{:S(2)}) collective-permute-start(bf16[1,112,340]{2,1,0:T(8,128)(2,1)S(1)} %get-tuple-element.25), channel_id=1, source_target_pairs={{0,4},{4,8},{8,12},{1,5},{5,9},{9,13},{2,6},{6,10},{10,14},{3,7},{... | collective-permute-start | bytes 228488 | tf_op jit(solution)/shard_map/ppermute | solution.py:17
  83.1 7.2 %collective-permute-start.15 = (bf16[1,112,340]{2,1,0:T(8,128)(2,1)S(1)}, bf16[1,112,340]{2,1,0:T(8,128)(2,1)S(1)}, u32[]{:S(2)}, u32[]{:S(2)}) collective-permute-start(bf16[1,112,340]{2,1,0:T(8,128)(2,1)S(1)} %get-tuple-element.26), channel_id=1, source_target_pairs={{4,0},{8,4},{12,8},{5,1},{9,5},{13,9},{6,2},{10,6},{14,10},{7,3},{... | collective-permute-start | bytes 228488 | tf_op jit(solution)/shard_map/ppermute | solution.py:19
  85.0 5.2 %collective-permute-start.13 = (bf16[1,112,340]{2,1,0:T(8,128)(2,1)S(1)}, bf16[1,112,340]{2,1,0:T(8,128)(2,1)S(1)}, u32[]{:S(2)}, u32[]{:S(2)}) collective-permute-start(bf16[1,112,340]{2,1,0:T(8,128)(2,1)S(1)} %get-tuple-element.28), channel_id=1, source_target_pairs={{16,0},{17,1},{18,2},{19,3},{20,4},{21,5},{22,6},{23,7},{24,8},{25... | collective-permute-start | bytes 228488 | tf_op jit(solution)/shard_map/ppermute | solution.py:19
  91.1 3.3 %copy-start.2 = (bf16[6,112,340]{2,1,0:T(8,128)(2,1)S(1)}, bf16[6,112,340]{2,1,0:T(8,128)(2,1)}, u32[]{:S(2)}) copy-start(bf16[6,112,340]{2,1,0:T(8,128)(2,1)} %copy-done.1) | copy-start | bytes 1370884
where the time goes:
time: 103 us; the launch traced here: 102 us
  starting transfers between devices  48 us (47%)
  matrix products  25.6 us (25%)
  local copies, waits for them, and re-layouts  13.8 us (13%)
  waiting for transfers between devices  11.6 us (11%)
  other arithmetic  1.55 us (2%)
  between operations  1.34 us (1%)
    ppermute x9, starting transfers between devices, with_halo(): lax.ppermute(tail, axis, [(i, (i + 1) % count) for i in range(ends)])  34.3 us
    dot_general x3, matrix products, local(): jnp.dot(lowered, operator, preferred_element_type=jnp.float32)  14.3 us
    ppermute x9, starting transfers between devices, with_halo(): lax.ppermute(head, axis, [((i + 1) % count, i) for i in range(ends)])  13.7 us
    ppermute x9, waiting for transfers between devices, with_halo(): lax.ppermute(head, axis, [((i + 1) % count, i) for i in range(ends)])  11.6 us
    concatenate x6, local copies, waits for them, and re-layouts, local(): jnp.concatenate([fresh[number] for number in range(6)] + [hidden[:, span:...  7.77 us
    dot_general x1, matrix products, local(): jnp.einsum('kij,kig->kjg', selector, gradient, precision=lax.Precision.HI...  4.77 us
    unnamed x66, local copies, waits for them, and re-layouts  4.6 us
    dot_general x1, matrix products, local(): jnp.einsum('kcf,kcg->kfg', jnp.concatenate(inputs_kept, axis=1), jnp.conc...  2.67 us
  transfers between devices with their start and end apart: 18, of which 3 were waited for; matrix products, arithmetic and copies ran while one was open for 5% of the time, Pallas kernels for 0%

commit v1 on v0

v1 whole, which is shorter than its diff:
```python
import functools
import math

import jax
import jax.numpy as jnp
from jax import lax
from jax.experimental import pallas as pl
from jax.experimental.pallas import tpu as pltpu
from jax.sharding import PartitionSpec as P

LANES = 128
BLOCK = 256
AXES = ("gx", "gy", "gz")


def up(value, step):
    return -(-value // step) * step


def kernel(
    width, seed_hbm, op_hbm, m_hbm, saved_hbm, map_ref, flag_ref, out_hbm, grad_hbm,
    seed_v, op_v, m_v, saved_v, map_v, sel_v, w_v, send_v, recv_v, inp_v, mapped_v, packed_v,
    hid_v, acc_v, st_v, stb_v, g_v, out_v, gout_v,
    in_sem, out_sem, send_sem, recv_sem,
):
    columns, trace = seed_v.shape
    sweeps = saved_v.shape[0]
    pad = up(width, LANES)
    span = 6 * width
    scale = 1.0 / math.sqrt(columns)
    x_end = up(2 * width, BLOCK)
    z_start = (4 * width) // BLOCK * BLOCK
    chunks = ((z_start, trace), (0, x_end), (x_end, z_start))
    order = ((4, 5), (0, 1), (2, 3))

    where = [lax.axis_index(name) for name in AXES]
    has = []
    for axis, name in enumerate(AXES):
        has.append(where[axis] > 0)
        has.append(where[axis] < lax.axis_size(name) - 1)

    def peer(face):
        return {AXES[face // 2]: where[face // 2] + (1 if face % 2 else -1)}

    def span_of(face):
        base = face * width // LANES * LANES
        shift = face * width - base
        return base, shift, up(shift + width, LANES)

    barrier = pltpu.get_barrier_semaphore()
    count = 0
    for face in range(6):
        @pl.when(has[face])
        def _(face=face):
            pl.semaphore_signal(
                barrier, inc=1, device_id=peer(face), device_id_type=pl.DeviceIdType.MESH
            )
        count = count + has[face].astype(jnp.int32)

    seed_in = pltpu.make_async_copy(seed_hbm, seed_v, in_sem.at[0])
    seed_in.start()
    op_in = []
    for number, (start, stop) in enumerate(chunks):
        copy = pltpu.make_async_copy(
            op_hbm.at[:, start:stop], op_v.at[:, start:stop], in_sem.at[1 + number]
        )
        copy.start()
        op_in.append(copy)
    m_in = pltpu.make_async_copy(m_hbm, m_v, in_sem.at[4])
    m_in.start()
    saved_in = pltpu.make_async_copy(saved_hbm, saved_v, in_sem.at[5])
    saved_in.start()

    for face in range(6):
        @pl.when(jnp.logical_not(has[face]))
        def _(face=face):
            for sweep in range(sweeps):
                recv_v[sweep, face] = jnp.zeros((columns, pad), jnp.bfloat16)

    map_v[...] = jnp.full(map_v.shape, -1, jnp.int32)
    map_v[0:6, 0:width] = map_ref[...]
    rows = lax.broadcasted_iota(jnp.int32, (pad, pad), 0)
    lane = lax.broadcasted_iota(jnp.int32, (1, pad), 1)
    for face in range(6):
        flag = (flag_ref[face] == 1).astype(jnp.int32)
        row = map_v[face : face + 1, :]
        row = jnp.where(lane < width, row + (lane - row) * flag, -1)
        sel_v[face] = jnp.where(rows == row, 1.0, 0.0).astype(jnp.bfloat16)
        w_v[face] = jnp.zeros((pad, pad), jnp.bfloat16)

    def remote(sweep, face):
        return pltpu.make_async_remote_copy(
            src_ref=send_v.at[sweep, face],
            dst_ref=recv_v.at[sweep, face ^ 1],
            send_sem=send_sem.at[sweep, face],
            recv_sem=recv_sem.at[sweep, face ^ 1],
            device_id=peer(face),
            device_id_type=pl.DeviceIdType.MESH,
        )

    def arrival(sweep, face):
        return pltpu.make_async_remote_copy(
            src_ref=send_v.at[sweep, face],
            dst_ref=recv_v.at[sweep, face],
            send_sem=send_sem.at[sweep, face],
            recv_sem=recv_sem.at[sweep, face],
            device_id=peer(face),
            device_id_type=pl.DeviceIdType.MESH,
        )

    def take_face(value, shift):
        if shift:
            value = pltpu.roll(value, value.shape[1] - shift, 1)
        return value[:, :pad].astype(jnp.bfloat16)

    def dot(left, right):
        return jnp.dot(left, right, preferred_element_type=jnp.float32)

    def emit(sweep, number):
        for face in order[number]:
            base, shift, extent = span_of(face)
            send_v[sweep, face] = take_face(hid_v[:, base : base + extent], shift)

            @pl.when(has[face])
            def _(face=face):
                remote(sweep, face).start()

    def absorb(sweep, number):
        for face in order[number]:
            @pl.when(has[face])
            def _(face=face):
                arrival(sweep, face).wait_recv()

            inputs = lax.select(flag_ref[face] == 1, send_v[sweep, face], recv_v[sweep, face])
            inp_v[sweep, face] = inputs
            fresh = dot(inputs, w_v[face])
            base, shift, extent = span_of(face)
            if extent > pad:
                fresh = jnp.concatenate(
                    [fresh, jnp.zeros((columns, extent - pad), jnp.float32)], axis=1
                )
            if shift:
                fresh = pltpu.roll(fresh, shift, 1)
            st_v[:, base : base + extent] += fresh

    def map_inputs(sweep):
        for face in range(6):
            mapped_v[face, sweep * columns : (sweep + 1) * columns, :] = dot(
                inp_v[sweep, face], sel_v[face]
            ).astype(jnp.bfloat16)

    def outer(face, start, stop):
        return lax.dot_general(
            mapped_v[face, start:stop, :],
            packed_v[face, start:stop, :],
            (((0,), (0,)), ((), ())),
            preferred_element_type=jnp.float32,
        )

    seed_in.wait()
    for sweep in range(sweeps):
        last = sweep == sweeps - 1
        for number, (start, stop) in enumerate(chunks):
            if sweep == 0:
                op_in[number].wait()
                hidden = dot(seed_v[...], op_v[:, start:stop])
            else:
                hidden = acc_v[:, start:stop] + dot(stb_v[:, 0:x_end], op_v[0:x_end, start:stop])
            hid_v[:, start:stop] = hidden
            if sweep == 0 and number == 0:
                pl.semaphore_wait(barrier, count)
            emit(sweep, number)

        if sweep == 0:
            m_in.wait()
            for face in range(6):
                w_v[face, :, 0:width] = dot(sel_v[face, :, 0:width], m_v[face]).astype(jnp.bfloat16)
        if sweep == 1:
            saved_in.wait()
            for face in range(6):
                base, shift, extent = span_of(face)
                for step in range(sweeps):
                    packed_v[face, step * columns : (step + 1) * columns, :] = take_face(
                        saved_v[sweeps - 1 - step, :, base : base + extent].astype(jnp.float32), shift
                    )
        if sweep >= 1:
            map_inputs(sweep - 1)
        if last:
            for face in range(6):
                g_v[face] = outer(face, 0, sweep * columns)

        st_v[...] = seed_v[...].astype(jnp.float32)
        tail = hid_v[:, trace - LANES : trace].astype(jnp.bfloat16).astype(jnp.float32)
        place = lax.broadcasted_iota(jnp.int32, (columns, LANES), 1) + (trace - LANES)
        st_v[:, trace - LANES : trace] += jnp.where(place >= span, tail, 0.0)
        for number in (2, 0, 1):
            absorb(sweep, number)
            start, stop = chunks[number]
            if not last:
                stb_v[:, start:stop] = st_v[:, start:stop].astype(jnp.bfloat16)
                if number == 2:
                    acc_v[...] = dot(stb_v[:, start:stop], op_v[start:stop, :])
                elif number == 0:
                    acc_v[...] += dot(stb_v[:, start:stop], op_v[start:stop, :])

    out_v[...] = st_v[...].astype(jnp.bfloat16)
    out_copy = pltpu.make_async_copy(out_v, out_hbm, out_sem.at[6])
    out_copy.start()
    map_inputs(sweeps - 1)
    grad_out = []
    for face in range(6):
        total = g_v[face] + outer(face, (sweeps - 1) * columns, sweeps * columns)
        gout_v[face] = (total * scale).astype(jnp.bfloat16)[0:width, 0:width]
        copy = pltpu.make_async_copy(gout_v.at[face], grad_hbm.at[face], out_sem.at[face])
        copy.start()
        grad_out.append(copy)
    for sweep in range(sweeps):
        for face in range(6):
            @pl.when(has[face])
            def _(face=face, sweep=sweep):
                remote(sweep, face).wait_send()
    out_copy.wait()
    for copy in grad_out:
        copy.wait()


def local(seed_cotangent, trace_operator, face_matrices, saved_traces, edge_flags, node_map):
    seed, operator, matrices, stored, flags, mapping = (
        array.reshape(array.shape[3:])
        for array in (
            seed_cotangent, trace_operator, face_matrices, saved_traces, edge_flags, node_map
        )
    )
    width = matrices.shape[-1]
    sweeps, columns, trace = stored.shape
    pad = up(width, LANES)
    bf16, f32 = jnp.bfloat16, jnp.float32
    anywhere = pl.BlockSpec(memory_space=pl.ANY)
    adjoint, gradient = pl.pallas_call(
        functools.partial(kernel, width),
        out_shape=(
            jax.ShapeDtypeStruct(seed.shape, bf16),
            jax.ShapeDtypeStruct(matrices.shape, bf16),
        ),
        in_specs=[anywhere] * 4
        + [pl.BlockSpec(memory_space=pltpu.VMEM), pl.BlockSpec(memory_space=pltpu.SMEM)],
        out_specs=(anywhere, anywhere),
        scratch_shapes=[
            pltpu.VMEM(seed.shape, bf16),
            pltpu.VMEM(operator.shape, bf16),
            pltpu.VMEM(matrices.shape, bf16),
            pltpu.VMEM(stored.shape, bf16),
            pltpu.VMEM((8, pad), jnp.int32),
            pltpu.VMEM((6, pad, pad), bf16),
            pltpu.VMEM((6, pad, pad), bf16),
            pltpu.VMEM((sweeps, 6, columns, pad), bf16),
            pltpu.VMEM((sweeps, 6, columns, pad), bf16),
            pltpu.VMEM((sweeps, 6, columns, pad), bf16),
            pltpu.VMEM((6, sweeps * columns, pad), bf16),
            pltpu.VMEM((6, sweeps * columns, pad), bf16),
            pltpu.VMEM(seed.shape, f32),
            pltpu.VMEM(seed.shape, f32),
            pltpu.VMEM(seed.shape, f32),
            pltpu.VMEM(seed.shape, bf16),
            pltpu.VMEM((6, pad, pad), f32),
            pltpu.VMEM(seed.shape, bf16),
            pltpu.VMEM(matrices.shape, bf16),
            pltpu.SemaphoreType.DMA((6,)),
            pltpu.SemaphoreType.DMA((7,)),
            pltpu.SemaphoreType.DMA((sweeps, 6)),
            pltpu.SemaphoreType.DMA((sweeps, 6)),
        ],
        compiler_params=pltpu.CompilerParams(
            collective_id=0, has_side_effects=True, vmem_limit_bytes=56 * 1024 * 1024
        ),
    )(seed, operator, matrices, stored, mapping, flags)
    return adjoint[None, None, None], gradient[None, None, None]


def solution(mesh):
    return jax.shard_map(
        local,
        mesh=mesh,
        in_specs=(
            P("gx", "gy", "gz", None, None),
            P("gx", "gy", "gz", None, None),
            P("gx", "gy", "gz", None, None, None),
            P("gx", "gy", "gz", None, None, None),
            P("gx", "gy", "gz", None),
            P("gx", "gy", "gz", None, None),
        ),
        out_specs=(P("gx", "gy", "gz", None, None), P("gx", "gy", "gz", None, None, None)),
        check_vma=False,
    )
```

time: 103 us -> 33.4 us (0.32)
  starting transfers between devices: 48 us -> 0 us
  Pallas kernels: 0 us -> 26.6 us
  matrix products: 25.6 us -> 0 us
  waiting for transfers between devices: 11.6 us -> 0 us
  local copies, waits for them, and re-layouts: 13.8 us -> 5.84 us
  other arithmetic: 1.55 us -> 0 us
    ppermute x18 -> x0, starting transfers between devices: 48 us -> none  [the longest x9 34.3 us: with_halo(): lax.ppermute(tail, axis, [(i, (i + 1) % count) for i in range(ends)])]
    pallas_call x0 -> x1, Pallas kernels: none -> 26.6 us  [local(): pl.pallas_call(functools.partial(kernel, width), out_shape=(jax.ShapeDtyp...]
    dot_general x9 -> x0, matrix products: 25.6 us -> none  [the longest x3 14.3 us: local(): jnp.dot(lowered, operator, preferred_element_type=jnp.float32)]
    ppermute x18 -> x0, waiting for transfers between devices: 11.6 us -> none  [the longest x9 11.6 us: with_halo(): lax.ppermute(head, axis, [((i + 1) % count, i) for i in range(ends)])]
    concatenate x6 -> x0, local copies, waits for them, and re-layouts: 7.77 us -> none  [local(): jnp.concatenate([fresh[number] for number in range(6)] + [hidden[:, span:...]
    another operation x11 -> x0, local copies, waits for them, and re-layouts: 1.26 us -> none  [the longest x6 0.98 us: local(): jnp.stack([face_block(hidden, number, width) for number in range(6)], axi...]
    unnamed x66 -> x3, local copies, waits for them, and re-layouts: 4.6 us -> 5.84 us
  transfers between devices with their start and end apart: 18 -> 0, of which waited for: 3 -> 0; matrix products, arithmetic and copies ran while one was open for 5% -> 0% of each run, Pallas kernels for 0% -> 0%
where the time goes in v1:
time: 33.4 us; the launch traced here: 33.1 us
  Pallas kernels  26.6 us (80%)
  local copies, waits for them, and re-layouts  5.84 us (17%)
  between operations  0.64 us (2%)
    pallas_call x1, Pallas kernels, local(): pl.pallas_call(functools.partial(kernel, width), out_shape=(jax.ShapeDtyp...  26.6 us
    unnamed x3, local copies, waits for them, and re-layouts  5.84 us

profile of v1, /device:TPU:1, one launch (start us, length us, event | category | flops | bytes accessed | tf_op | source)
XLA Modules:
  0.0 33.1 jit_solution(15382092450644697144)
XLA Ops:
  0.6 1.3 %copy.10 = s32[1,1,1,6,340]{4,3,2,1,0:T(8,128)} copy(s32[1,1,1,6,340]{4,2,3,1,0:T(1,128)} %param.11) | data formatting | bytes 16320
  1.9 26.6 %shard_map.77 = (bf16[112,2048]{1,0:T(8,128)(2,1)}, bf16[6,340,340]{2,1,0:T(8,128)(2,1)}) custom-call(bf16[112,2048]{1,0:T(8,128)(2,1)} %bitcast.15, bf16[2048,2048]{1,0:T(8,128)(2,1)} %bitcast.10, bf16[6,340,340]{2,1,0:T(8,128)(2,1)} %bitcast.12, bf16[3,112,2048]{2,1,0:T(8,128)(2,1)} %bitcast.13, s32[6,340]{1,0:T(8,128)} %bitcast.16, s32[6]{0:T(128)} %bitcast.17), custom_call_target="tpu_custom_call" | custom-call | tf_op jit(solution)/shard_map/pallas_call | solution.py:239
  28.6 1.8 %copy.13 = bf16[1,1,1,112,2048]{4,3,2,1,0:T(8,128)(2,1)} copy(bf16[1,1,1,112,2048]{4,3,2,1,0:T(8,128)(2,1)} %bitcast.14) | data formatting | bytes 917504
  30.4 2.7 %copy.14 = bf16[1,1,1,6,340,340]{5,4,3,2,1,0:T(8,128)(2,1)} copy(bf16[1,1,1,6,340,340]{5,4,3,2,1,0:T(8,128)(2,1)} %bitcast.11) | data formatting | bytes 2774400

commit v2 on v1

--- a/solution.py
+++ b/solution.py
@@ -18,10 +18,10 @@
 
 
 def kernel(
-    width, seed_hbm, op_hbm, m_hbm, saved_hbm, map_ref, flag_ref, out_hbm, grad_hbm,
+    width, seed_hbm, op_hbm, m_hbm, saved_hbm, map_hbm, flag_ref, out_ref, grad_ref,
     seed_v, op_v, m_v, saved_v, map_v, sel_v, w_v, send_v, recv_v, inp_v, mapped_v, packed_v,
-    hid_v, acc_v, st_v, stb_v, g_v, out_v, gout_v,
-    in_sem, out_sem, send_sem, recv_sem,
+    hid_v, acc_v, st_v, stb_v, g_v,
+    in_sem, send_sem, recv_sem,
 ):
     columns, trace = seed_v.shape
     sweeps = saved_v.shape[0]
@@ -66,6 +66,8 @@
         )
         copy.start()
         op_in.append(copy)
+    map_in = pltpu.make_async_copy(map_hbm, map_v, in_sem.at[6])
+    map_in.start()
     m_in = pltpu.make_async_copy(m_hbm, m_v, in_sem.at[4])
     m_in.start()
     saved_in = pltpu.make_async_copy(saved_hbm, saved_v, in_sem.at[5])
@@ -76,17 +78,6 @@
         def _(face=face):
             for sweep in range(sweeps):
                 recv_v[sweep, face] = jnp.zeros((columns, pad), jnp.bfloat16)
-
-    map_v[...] = jnp.full(map_v.shape, -1, jnp.int32)
-    map_v[0:6, 0:width] = map_ref[...]
-    rows = lax.broadcasted_iota(jnp.int32, (pad, pad), 0)
-    lane = lax.broadcasted_iota(jnp.int32, (1, pad), 1)
-    for face in range(6):
-        flag = (flag_ref[face] == 1).astype(jnp.int32)
-        row = map_v[face : face + 1, :]
-        row = jnp.where(lane < width, row + (lane - row) * flag, -1)
-        sel_v[face] = jnp.where(rows == row, 1.0, 0.0).astype(jnp.bfloat16)
-        w_v[face] = jnp.zeros((pad, pad), jnp.bfloat16)
 
     def remote(sweep, face):
         return pltpu.make_async_remote_copy(
@@ -120,7 +111,7 @@
         for face in order[number]:
             base, shift, extent = span_of(face)
             send_v[sweep, face] = take_face(hid_v[:, base : base + extent], shift)
-
+        for face in order[number]:
             @pl.when(has[face])
             def _(face=face):
                 remote(sweep, face).start()
@@ -131,6 +122,7 @@
             def _(face=face):
                 arrival(sweep, face).wait_recv()
 
+        for face in order[number]:
             inputs = lax.select(flag_ref[face] == 1, send_v[sweep, face], recv_v[sweep, face])
             inp_v[sweep, face] = inputs
             fresh = dot(inputs, w_v[face])
@@ -143,8 +135,8 @@
                 fresh = pltpu.roll(fresh, shift, 1)
             st_v[:, base : base + extent] += fresh
 
-    def map_inputs(sweep):
-        for face in range(6):
+    def map_inputs(sweep, faces=range(6)):
+        for face in faces:
             mapped_v[face, sweep * columns : (sweep + 1) * columns, :] = dot(
                 inp_v[sweep, face], sel_v[face]
             ).astype(jnp.bfloat16)
@@ -172,6 +164,18 @@
             emit(sweep, number)
 
         if sweep == 0:
+            map_in.wait()
+            rows = lax.broadcasted_iota(jnp.int32, (pad, width), 0).astype(jnp.int16)
+            lane = lax.broadcasted_iota(jnp.int32, (1, width), 1)
+            for face in range(6):
+                flag = (flag_ref[face] == 1).astype(jnp.int32)
+                row = map_v[face]
+                row = row + (lane - row) * flag
+                sel_v[face, :, width:pad] = jnp.zeros((pad, pad - width), jnp.bfloat16)
+                sel_v[face, :, 0:width] = jnp.where(
+                    rows == row.astype(jnp.int16), jnp.bfloat16(1.0), jnp.bfloat16(0.0)
+                )
+                w_v[face, :, width:pad] = jnp.zeros((pad, pad - width), jnp.bfloat16)
             m_in.wait()
             for face in range(6):
                 w_v[face, :, 0:width] = dot(sel_v[face, :, 0:width], m_v[face]).astype(jnp.bfloat16)
@@ -196,32 +200,24 @@
         for number in (2, 0, 1):
             absorb(sweep, number)
             start, stop = chunks[number]
-            if not last:
+            if last:
+                map_inputs(sweep, order[number])
+                for face in order[number]:
+                    total = g_v[face] + outer(face, sweep * columns, (sweep + 1) * columns)
+                    grad_ref[face] = (total * scale).astype(jnp.bfloat16)[0:width, 0:width]
+            else:
                 stb_v[:, start:stop] = st_v[:, start:stop].astype(jnp.bfloat16)
                 if number == 2:
                     acc_v[...] = dot(stb_v[:, start:stop], op_v[start:stop, :])
                 elif number == 0:
                     acc_v[...] += dot(stb_v[:, start:stop], op_v[start:stop, :])
 
-    out_v[...] = st_v[...].astype(jnp.bfloat16)
-    out_copy = pltpu.make_async_copy(out_v, out_hbm, out_sem.at[6])
-    out_copy.start()
-    map_inputs(sweeps - 1)
-    grad_out = []
-    for face in range(6):
-        total = g_v[face] + outer(face, (sweeps - 1) * columns, sweeps * columns)
-        gout_v[face] = (total * scale).astype(jnp.bfloat16)[0:width, 0:width]
-        copy = pltpu.make_async_copy(gout_v.at[face], grad_hbm.at[face], out_sem.at[face])
-        copy.start()
-        grad_out.append(copy)
+    out_ref[...] = st_v[...].astype(jnp.bfloat16)
     for sweep in range(sweeps):
         for face in range(6):
             @pl.when(has[face])
             def _(face=face, sweep=sweep):
                 remote(sweep, face).wait_send()
-    out_copy.wait()
-    for copy in grad_out:
-        copy.wait()
 
 
 def local(seed_cotangent, trace_operator, face_matrices, saved_traces, edge_flags, node_map):
@@ -235,22 +231,23 @@
     sweeps, columns, trace = stored.shape
     pad = up(width, LANES)
     bf16, f32 = jnp.bfloat16, jnp.float32
-    anywhere = pl.BlockSpec(memory_space=pl.ANY)
+    anywhere = pl.BlockSpec(memory_space=pltpu.HBM)
+    resident = pl.BlockSpec(memory_space=pltpu.VMEM)
     adjoint, gradient = pl.pallas_call(
         functools.partial(kernel, width),
         out_shape=(
             jax.ShapeDtypeStruct(seed.shape, bf16),
             jax.ShapeDtypeStruct(matrices.shape, bf16),
         ),
-        in_specs=[anywhere] * 4
-        + [pl.BlockSpec(memory_space=pltpu.VMEM), pl.BlockSpec(memory_space=pltpu.SMEM)],
-        out_specs=(anywhere, anywhere),
+        in_specs=[anywhere] * 5
+        + [pl.BlockSpec(memory_space=pltpu.SMEM)],
+        out_specs=(resident, resident),
         scratch_shapes=[
             pltpu.VMEM(seed.shape, bf16),
             pltpu.VMEM(operator.shape, bf16),
             pltpu.VMEM(matrices.shape, bf16),
             pltpu.VMEM(stored.shape, bf16),
-            pltpu.VMEM((8, pad), jnp.int32),
+            pltpu.VMEM((6, 1, width), jnp.int32),
             pltpu.VMEM((6, pad, pad), bf16),
             pltpu.VMEM((6, pad, pad), bf16),
             pltpu.VMEM((sweeps, 6, columns, pad), bf16),
@@ -263,17 +260,14 @@
             pltpu.VMEM(seed.shape, f32),
             pltpu.VMEM(seed.shape, bf16),
             pltpu.VMEM((6, pad, pad), f32),
-            pltpu.VMEM(seed.shape, bf16),
-            pltpu.VMEM(matrices.shape, bf16),
-            pltpu.SemaphoreType.DMA((6,)),
             pltpu.SemaphoreType.DMA((7,)),
             pltpu.SemaphoreType.DMA((sweeps, 6)),
             pltpu.SemaphoreType.DMA((sweeps, 6)),
         ],
         compiler_params=pltpu.CompilerParams(
-            collective_id=0, has_side_effects=True, vmem_limit_bytes=56 * 1024 * 1024
+            collective_id=0, has_side_effects=True, vmem_limit_bytes=40 * 1024 * 1024
         ),
-    )(seed, operator, matrices, stored, mapping, flags)
+    )(*(pltpu.with_memory_space_constraint(array, pltpu.HBM) for array in (seed, operator, matrices, stored, mapping[:, None, :], flags)))
     return adjoint[None, None, None], gradient[None, None, None]
 
 

time: 33.4 us -> 27.1 us (0.81)
  local copies, waits for them, and re-layouts: 5.84 us -> 1.92 us
  Pallas kernels: 26.6 us -> 24.4 us
    unnamed x3 -> x2, local copies, waits for them, and re-layouts: 5.84 us -> 1.92 us
    pallas_call x1, Pallas kernels: 26.6 us -> 24.4 us  [local(): pl.pallas_call(functools.partial(kernel, width), out_shape=(jax.ShapeDtyp...]
where the time goes in v2:
time: 27.1 us; the launch traced here: 27 us
  Pallas kernels  24.4 us (90%)
  local copies, waits for them, and re-layouts  1.92 us (7%)
  between operations  0.64 us (2%)
    pallas_call x1, Pallas kernels, local(): pl.pallas_call(functools.partial(kernel, width), out_shape=(jax.ShapeDtyp...  24.4 us
    unnamed x2, local copies, waits for them, and re-layouts  1.92 us

profile of v2, /device:TPU:1, one launch (start us, length us, event | category | flops | bytes accessed | tf_op | source)
XLA Modules:
  0.0 27.0 jit_solution(16506464349434799333)
XLA Ops:
  0.6 24.4 %shard_map.77 = (bf16[112,2048]{1,0:T(8,128)(2,1)S(1)}, bf16[6,340,340]{2,1,0:T(8,128)(2,1)S(1)}) custom-call(bf16[112,2048]{1,0:T(8,128)(2,1)} %bitcast.13, bf16[2048,2048]{1,0:T(8,128)(2,1)} %bitcast.10, bf16[6,340,340]{2,1,0:T(8,128)(2,1)} %bitcast.11, bf16[3,112,2048]{2,1,0:T(8,128)(2,1)} %bitcast.12, s32[6,1,340]{2,1,0:T(1,128)} %bitcast.14, s32[6]{0:T(128)} %bitcast.15), custom_call_target="tpu_custom_call" | custom-call | tf_op jit(solution)/shard_map/pallas_call | solution.py:236
  25.1 0.8 %copy.10 = bf16[1,1,1,112,2048]{4,3,2,1,0:T(8,128)(2,1)} copy(bf16[1,1,1,112,2048]{4,3,2,1,0:T(8,128)(2,1)S(1)} %bitcast.9) | data formatting | bytes 917504
  25.8 1.1 %copy.11 = bf16[1,1,1,6,340,340]{5,4,3,2,1,0:T(8,128)(2,1)} copy(bf16[1,1,1,6,340,340]{5,4,3,2,1,0:T(8,128)(2,1)S(1)} %bitcast.8) | data formatting | bytes 2774400

commit v3 on v2

--- a/solution.py
+++ b/solution.py
@@ -19,7 +19,7 @@
 
 def kernel(
     width, seed_hbm, op_hbm, m_hbm, saved_hbm, map_hbm, flag_ref, out_ref, grad_ref,
-    seed_v, op_v, m_v, saved_v, map_v, sel_v, w_v, send_v, recv_v, inp_v, mapped_v, packed_v,
+    seed_v, op_v, m_v, saved_v, map_v, sel_v, w_v, send_v, recv_v, mapped_v, packed_v,
     hid_v, acc_v, st_v, stb_v, g_v,
     in_sem, send_sem, recv_sem,
 ):
@@ -57,6 +57,8 @@
             )
         count = count + has[face].astype(jnp.int32)
 
+    map_in = pltpu.make_async_copy(map_hbm, map_v, in_sem.at[6])
+    map_in.start()
     seed_in = pltpu.make_async_copy(seed_hbm, seed_v, in_sem.at[0])
     seed_in.start()
     op_in = []
@@ -66,8 +68,6 @@
         )
         copy.start()
         op_in.append(copy)
-    map_in = pltpu.make_async_copy(map_hbm, map_v, in_sem.at[6])
-    map_in.start()
     m_in = pltpu.make_async_copy(m_hbm, m_v, in_sem.at[4])
     m_in.start()
     saved_in = pltpu.make_async_copy(saved_hbm, saved_v, in_sem.at[5])
@@ -124,8 +124,9 @@
 
         for face in order[number]:
             inputs = lax.select(flag_ref[face] == 1, send_v[sweep, face], recv_v[sweep, face])
-            inp_v[sweep, face] = inputs
-            fresh = dot(inputs, w_v[face])
+            mapped = dot(inputs, sel_v[face]).astype(jnp.bfloat16)
+            mapped_v[face, sweep * columns : (sweep + 1) * columns, :] = mapped
+            fresh = dot(mapped, w_v[face])
             base, shift, extent = span_of(face)
             if extent > pad:
                 fresh = jnp.concatenate(
@@ -135,12 +136,6 @@
                 fresh = pltpu.roll(fresh, shift, 1)
             st_v[:, base : base + extent] += fresh
 
-    def map_inputs(sweep, faces=range(6)):
-        for face in faces:
-            mapped_v[face, sweep * columns : (sweep + 1) * columns, :] = dot(
-                inp_v[sweep, face], sel_v[face]
-            ).astype(jnp.bfloat16)
-
     def outer(face, start, stop):
         return lax.dot_general(
             mapped_v[face, start:stop, :],
@@ -149,6 +144,18 @@
             preferred_element_type=jnp.float32,
         )
 
+    map_in.wait()
+    rows = lax.broadcasted_iota(jnp.int32, (pad, width), 0).astype(jnp.int16)
+    lane = lax.broadcasted_iota(jnp.int32, (1, width), 1)
+    for face in range(6):
+        flag = (flag_ref[face] == 1).astype(jnp.int32)
+        row = map_v[face]
+        row = row + (lane - row) * flag
+        sel_v[face, :, width:pad] = jnp.zeros((pad, pad - width), jnp.bfloat16)
+        sel_v[face, :, 0:width] = jnp.where(
+            rows == row.astype(jnp.int16), jnp.bfloat16(1.0), jnp.bfloat16(0.0)
+        )
+        w_v[face] = jnp.zeros((pad, pad), jnp.bfloat16)
     seed_in.wait()
     for sweep in range(sweeps):
         last = sweep == sweeps - 1
@@ -164,22 +171,9 @@
             emit(sweep, number)
 
         if sweep == 0:
-            map_in.wait()
-            rows = lax.broadcasted_iota(jnp.int32, (pad, width), 0).astype(jnp.int16)
-            lane = lax.broadcasted_iota(jnp.int32, (1, width), 1)
-            for face in range(6):
-                flag = (flag_ref[face] == 1).astype(jnp.int32)
-                row = map_v[face]
-                row = row + (lane - row) * flag
-                sel_v[face, :, width:pad] = jnp.zeros((pad, pad - width), jnp.bfloat16)
-                sel_v[face, :, 0:width] = jnp.where(
-                    rows == row.astype(jnp.int16), jnp.bfloat16(1.0), jnp.bfloat16(0.0)
-                )
-                w_v[face, :, width:pad] = jnp.zeros((pad, pad - width), jnp.bfloat16)
             m_in.wait()
             for face in range(6):
-                w_v[face, :, 0:width] = dot(sel_v[face, :, 0:width], m_v[face]).astype(jnp.bfloat16)
-        if sweep == 1:
+                w_v[face, 0:width, 0:width] = m_v[face]
             saved_in.wait()
             for face in range(6):
                 base, shift, extent = span_of(face)
@@ -187,8 +181,6 @@
                     packed_v[face, step * columns : (step + 1) * columns, :] = take_face(
                         saved_v[sweeps - 1 - step, :, base : base + extent].astype(jnp.float32), shift
                     )
-        if sweep >= 1:
-            map_inputs(sweep - 1)
         if last:
             for face in range(6):
                 g_v[face] = outer(face, 0, sweep * columns)
@@ -201,7 +193,6 @@
             absorb(sweep, number)
             start, stop = chunks[number]
             if last:
-                map_inputs(sweep, order[number])
                 for face in order[number]:
                     total = g_v[face] + outer(face, sweep * columns, (sweep + 1) * columns)
                     grad_ref[face] = (total * scale).astype(jnp.bfloat16)[0:width, 0:width]
@@ -252,7 +243,6 @@
             pltpu.VMEM((6, pad, pad), bf16),
             pltpu.VMEM((sweeps, 6, columns, pad), bf16),
             pltpu.VMEM((sweeps, 6, columns, pad), bf16),
-            pltpu.VMEM((sweeps, 6, columns, pad), bf16),
             pltpu.VMEM((6, sweeps * columns, pad), bf16),
             pltpu.VMEM((6, sweeps * columns, pad), bf16),
             pltpu.VMEM(seed.shape, f32),

time: 27.1 us -> 29.5 us (1.089)
  Pallas kernels: 24.4 us -> 26.7 us
    pallas_call x1, Pallas kernels: 24.4 us -> 26.7 us  [local(): pl.pallas_call(functools.partial(kernel, width), out_shape=(jax.ShapeDtyp...]
where the time goes in v3:
time: 29.5 us; the launch traced here: 29.3 us
  Pallas kernels  26.7 us (91%)
  local copies, waits for them, and re-layouts  1.92 us (7%)
  between operations  0.64 us (2%)
    pallas_call x1, Pallas kernels, local(): pl.pallas_call(functools.partial(kernel, width), out_shape=(jax.ShapeDtyp...  26.7 us
    unnamed x2, local copies, waits for them, and re-layouts  1.92 us

profile of v3, /device:TPU:1, one launch (start us, length us, event | category | flops | bytes accessed | tf_op | source)
XLA Modules:
  0.0 29.3 jit_solution(11873639188857501191)
XLA Ops:
  0.6 26.7 %shard_map.77 = (bf16[112,2048]{1,0:T(8,128)(2,1)S(1)}, bf16[6,340,340]{2,1,0:T(8,128)(2,1)S(1)}) custom-call(bf16[112,2048]{1,0:T(8,128)(2,1)} %bitcast.13, bf16[2048,2048]{1,0:T(8,128)(2,1)} %bitcast.10, bf16[6,340,340]{2,1,0:T(8,128)(2,1)} %bitcast.11, bf16[3,112,2048]{2,1,0:T(8,128)(2,1)} %bitcast.12, s32[6,1,340]{2,1,0:T(1,128)} %bitcast.14, s32[6]{0:T(128)} %bitcast.15), custom_call_target="tpu_custom_call" | custom-call | tf_op jit(solution)/shard_map/pallas_call | solution.py:227
  27.4 0.8 %copy.10 = bf16[1,1,1,112,2048]{4,3,2,1,0:T(8,128)(2,1)} copy(bf16[1,1,1,112,2048]{4,3,2,1,0:T(8,128)(2,1)S(1)} %bitcast.9) | data formatting | bytes 917504
  28.1 1.1 %copy.11 = bf16[1,1,1,6,340,340]{5,4,3,2,1,0:T(8,128)(2,1)} copy(bf16[1,1,1,6,340,340]{5,4,3,2,1,0:T(8,128)(2,1)S(1)} %bitcast.8) | data formatting | bytes 2774400

commit v4 on v3

--- a/solution.py
+++ b/solution.py
@@ -19,7 +19,7 @@
 
 def kernel(
     width, seed_hbm, op_hbm, m_hbm, saved_hbm, map_hbm, flag_ref, out_ref, grad_ref,
-    seed_v, op_v, m_v, saved_v, map_v, sel_v, w_v, send_v, recv_v, mapped_v, packed_v,
+    seed_v, op_v, m_v, saved_v, map_v, sel_v, w_v, send_v, recv_v, inp_v, mapped_v, packed_v,
     hid_v, acc_v, st_v, stb_v, g_v,
     in_sem, send_sem, recv_sem,
 ):
@@ -124,9 +124,8 @@
 
         for face in order[number]:
             inputs = lax.select(flag_ref[face] == 1, send_v[sweep, face], recv_v[sweep, face])
-            mapped = dot(inputs, sel_v[face]).astype(jnp.bfloat16)
-            mapped_v[face, sweep * columns : (sweep + 1) * columns, :] = mapped
-            fresh = dot(mapped, w_v[face])
+            inp_v[sweep, face] = inputs
+            fresh = dot(inputs, w_v[face])
             base, shift, extent = span_of(face)
             if extent > pad:
                 fresh = jnp.concatenate(
@@ -135,6 +134,12 @@
             if shift:
                 fresh = pltpu.roll(fresh, shift, 1)
             st_v[:, base : base + extent] += fresh
+
+    def map_inputs(sweep, faces=range(6)):
+        for face in faces:
+            mapped_v[face, sweep * columns : (sweep + 1) * columns, :] = dot(
+                inp_v[sweep, face], sel_v[face]
+            ).astype(jnp.bfloat16)
 
     def outer(face, start, stop):
         return lax.dot_general(
@@ -155,7 +160,7 @@
         sel_v[face, :, 0:width] = jnp.where(
             rows == row.astype(jnp.int16), jnp.bfloat16(1.0), jnp.bfloat16(0.0)
         )
-        w_v[face] = jnp.zeros((pad, pad), jnp.bfloat16)
+        w_v[face, :, width:pad] = jnp.zeros((pad, pad - width), jnp.bfloat16)
     seed_in.wait()
     for sweep in range(sweeps):
         last = sweep == sweeps - 1
@@ -173,7 +178,8 @@
         if sweep == 0:
             m_in.wait()
             for face in range(6):
-                w_v[face, 0:width, 0:width] = m_v[face]
+                w_v[face, :, 0:width] = dot(sel_v[face, :, 0:width], m_v[face]).astype(jnp.bfloat16)
+        if sweep == 1:
             saved_in.wait()
             for face in range(6):
                 base, shift, extent = span_of(face)
@@ -181,6 +187,8 @@
                     packed_v[face, step * columns : (step + 1) * columns, :] = take_face(
                         saved_v[sweeps - 1 - step, :, base : base + extent].astype(jnp.float32), shift
                     )
+        if sweep >= 1:
+            map_inputs(sweep - 1)
         if last:
             for face in range(6):
                 g_v[face] = outer(face, 0, sweep * columns)
@@ -193,6 +201,7 @@
             absorb(sweep, number)
             start, stop = chunks[number]
             if last:
+                map_inputs(sweep, order[number])
                 for face in order[number]:
                     total = g_v[face] + outer(face, sweep * columns, (sweep + 1) * columns)
                     grad_ref[face] = (total * scale).astype(jnp.bfloat16)[0:width, 0:width]
@@ -243,6 +252,7 @@
             pltpu.VMEM((6, pad, pad), bf16),
             pltpu.VMEM((sweeps, 6, columns, pad), bf16),
             pltpu.VMEM((sweeps, 6, columns, pad), bf16),
+            pltpu.VMEM((sweeps, 6, columns, pad), bf16),
             pltpu.VMEM((6, sweeps * columns, pad), bf16),
             pltpu.VMEM((6, sweeps * columns, pad), bf16),
             pltpu.VMEM(seed.shape, f32),

time: 29.5 us -> 27.2 us (0.922)
  Pallas kernels: 26.7 us -> 24.4 us
    pallas_call x1, Pallas kernels: 26.7 us -> 24.4 us  [local(): pl.pallas_call(functools.partial(kernel, width), out_shape=(jax.ShapeDtyp...]
where the time goes in v4:
time: 27.2 us; the launch traced here: 27 us
  Pallas kernels  24.4 us (90%)
  local copies, waits for them, and re-layouts  1.92 us (7%)
  between operations  0.64 us (2%)
    pallas_call x1, Pallas kernels, local(): pl.pallas_call(functools.partial(kernel, width), out_shape=(jax.ShapeDtyp...  24.4 us
    unnamed x2, local copies, waits for them, and re-layouts  1.92 us

profile of v4, /device:TPU:1, one launch (start us, length us, event | category | flops | bytes accessed | tf_op | source)
XLA Modules:
  0.0 27.0 jit_solution(9968098193549388643)
XLA Ops:
  0.6 24.4 %shard_map.77 = (bf16[112,2048]{1,0:T(8,128)(2,1)S(1)}, bf16[6,340,340]{2,1,0:T(8,128)(2,1)S(1)}) custom-call(bf16[112,2048]{1,0:T(8,128)(2,1)} %bitcast.13, bf16[2048,2048]{1,0:T(8,128)(2,1)} %bitcast.10, bf16[6,340,340]{2,1,0:T(8,128)(2,1)} %bitcast.11, bf16[3,112,2048]{2,1,0:T(8,128)(2,1)} %bitcast.12, s32[6,1,340]{2,1,0:T(1,128)} %bitcast.14, s32[6]{0:T(128)} %bitcast.15), custom_call_target="tpu_custom_call" | custom-call | tf_op jit(solution)/shard_map/pallas_call | solution.py:236
  25.1 0.8 %copy.10 = bf16[1,1,1,112,2048]{4,3,2,1,0:T(8,128)(2,1)} copy(bf16[1,1,1,112,2048]{4,3,2,1,0:T(8,128)(2,1)S(1)} %bitcast.9) | data formatting | bytes 917504
  25.8 1.1 %copy.11 = bf16[1,1,1,6,340,340]{5,4,3,2,1,0:T(8,128)(2,1)} copy(bf16[1,1,1,6,340,340]{5,4,3,2,1,0:T(8,128)(2,1)S(1)} %bitcast.8) | data formatting | bytes 2774400
